TPU v7x, 256 devices: a whole 4x4x8 slice. The times are simulated.
256 devices in a mesh: pipe: 16 (over z, core), dp: 4 (over x), tensor: 4 (over y).
Axes of the slice: x: 4, y: 4, z: 8, core: 2. Of those that a mesh axis runs over, the one named last changes fastest.
Arguments:
- acts: bfloat16 [16, 2048, 8192], P('pipe', 'dp', 'tensor'), may hold values from -6 to 6
- grads: bfloat16 [16, 2048, 8192], P('pipe', 'dp', 'tensor'), may hold values from -6 to 6
- sketch_index: int32 [16, 2, 16], P('pipe'), may hold values from 0 to 63, as said below
- sketch_values: bfloat16 [16, 2, 16, 128, 32], P('pipe'), may hold values from -0.125 to 0.125
Outputs:
- basis: float32 [16384, 256], P(('pipe', 'tensor'), 'dp')
Inputs may be any that keep to these rules, and one draw needn't show every extreme that they name: `sketch_index`: the 16 blocks of each sketch are distinct.
All inputs are finite; a program needn't handle non-finite values.
Results may differ from a plain program's by a relative error of at most 0.0003.
Values sent between devices are 32-bit elements; how exact they have to be, the bound alone decides.
A program may use at most 64 MiB of HBM per device.

v0:
```python
import jax
import jax.numpy as jnp
from jax import lax
from jax.sharding import PartitionSpec as P

RANK = 256
ITERS = 2
TOK_EX = 4


def from_partner(block, axis, apart):
    count = lax.axis_size(axis)
    route = []
    for low in range(count):
        high = low | 1 << apart
        if high != low and high < count:
            route += [(low, high), (high, low)]
    return lax.ppermute(block, axis, route)


def mm(a, b):
    return jnp.matmul(a, b, precision=lax.Precision.HIGHEST)


def layer_total(value):
    return lax.psum(value, "pipe")


def orthonormal(block, total):
    lower = jnp.linalg.cholesky(total(mm(block.T, block)))
    return lax.linalg.triangular_solve(lower, block, left_side=False, lower=True, transpose_a=True)


def reduce_plain(joined, total):
    q_basis = orthonormal(joined[:, :RANK] + joined[:, RANK:], total)
    for turn in range(ITERS):
        q_basis = orthonormal(mm(joined, total(mm(joined.T, q_basis))), total)
    weights = total(mm(joined.T, q_basis))
    lower = jnp.linalg.cholesky(mm(weights.T, weights))
    return mm(q_basis, lower)


def shards(acts, grads, sketch_index, sketch_values):
    local_width = acts.shape[2]
    blocks = local_width // 128
    width = sketch_values.shape[4]
    tensor_pos = lax.axis_index("tensor")
    tensor_count = lax.axis_size("tensor")
    span = jnp.arange(blocks, dtype=jnp.int32) + tensor_pos * blocks
    onehot = (sketch_index[0][:, :, None] == span[None, None, :]).astype(jnp.bfloat16)
    local = jnp.einsum(
        "sij,sicd->sjcd", onehot, sketch_values[0], preferred_element_type=jnp.float32
    )
    local = local.astype(jnp.bfloat16).reshape(2, local_width, width)
    left_part = jnp.dot(acts[0], local[0], preferred_element_type=jnp.float32)
    right_part = jnp.dot(grads[0], local[1], preferred_element_type=jnp.float32)
    both = lax.psum(jnp.concatenate([left_part, right_part], axis=1), "tensor")
    left_all = both[:, :width].reshape(-1, TOK_EX, width)
    right_all = both[:, width:].reshape(-1, TOK_EX, width)
    outer = jnp.einsum("etk,etl->ekl", left_all, right_all, precision=lax.Precision.HIGHEST)
    current = outer.reshape(outer.shape[0], -1).T
    position = lax.axis_index("dp")
    for bit in range(lax.axis_size("dp").bit_length() - 1):
        partner = from_partner(current, "dp", bit)
        upper = jnp.right_shift(position, bit) % 2
        joined = jnp.where(
            upper == 0,
            jnp.concatenate([current, partner], axis=1),
            jnp.concatenate([partner, current], axis=1),
        )
        if joined.shape[1] <= RANK:
            current = joined
        else:
            current = reduce_plain(joined, layer_total)
    part_rows = current.shape[0] // tensor_count
    current = lax.dynamic_slice_in_dim(current, tensor_pos * part_rows, part_rows, 0)
    own_columns = current.shape[1] // lax.axis_size("dp")
    current = lax.dynamic_slice_in_dim(current, position * own_columns, own_columns, 1)
    return current


def solution(mesh):
    placed = (
        P("pipe", "dp", "tensor"),
        P("pipe", "dp", "tensor"),
        P("pipe", None, None),
        P("pipe", None, None, None, None),
    )
    return jax.shard_map(
        shards, mesh=mesh, in_specs=placed, out_specs=P(("pipe", "tensor"), "dp"), check_vma=False
    )
```

profile of v0, /device:TPU:1, one launch (start us, length us, event | category | flops | bytes accessed | tf_op | source)
XLA Modules:
  0.0 1064.1 jit_solution(16470218660606452282)
XLA Ops:
  10.4 48.4 %all-reduce.9.cloned.1.call-done = f32[512,64]{0,1:T(8,128)} async-done(((f32[512,64]{0,1:T(8,128)}), f32[512,64]{0,1:T(8,128)}) %all-reduce.9.cloned.1.call-update) | async-done | bytes 131088 | tf_op jit(solution)/shard_map/psum | solution.py:57
  60.0 4.8 fusion.84
  68.7 9.7 collective-permute-done
  82.8 20.0 %collective-permute-done.1 = f32[1024,256]{1,0:T(8,128)} collective-permute-done((f32[1024,256]{1,0:T(8,128)S(1)}, f32[1024,256]{1,0:T(8,128)}, u32[]{:S(2)}, u32[]{:S(2)}) %collective-permute-start.1) | collective-permute-done | bytes 1048608 | tf_op jit(solution)/shard_map/ppermute | solution.py:18
  109.0 114.7 %all-reduce.11.cloned.1.call-done = f32[256,256]{0,1:T(8,128)} async-done(((f32[256,256]{0,1:T(8,128)}), f32[256,256]{0,1:T(8,128)}) %all-reduce.11.cloned.1.call-update) | async-done | bytes 262160 | tf_op jit(solution)/shard_map/psum | solution.py:26
  226.5 11.7 %cholesky.214 = f32[128,128]{1,0:T(8,128)S(1)} custom-call(f32[128,128]{1,0:T(8,128)S(1)} %cholesky.346), custom_call_target="Cholesky" | custom-call | tf_op jit(solution)/shard_map/jit(cholesky)/cholesky | solution.py:30
  238.2 9.8 custom-call.16
  250.2 11.7 %cholesky.231 = f32[128,128]{1,0:T(8,128)S(1)} custom-call(f32[128,128]{1,0:T(8,128)S(1)} %convolution_subtract_fusion.3), custom_call_target="Cholesky" | custom-call | tf_op jit(solution)/shard_map/jit(cholesky)/cholesky | solution.py:30
  264.9 4.1 while.6
  269.6 20.5 %custom-call.17 = f32[2,128,128]{1,2,0:T(8,128)S(1)} custom-call(f32[2,128,128]{2,1,0:T(8,128)} %copy-done.18), custom_call_target="InvertDiagBlocksLowerTriangular" | custom-call | tf_op jit(solution)/shard_map/triangular_solve/custom-call.0 | solution.py:31
  292.5 4.3 fusion.10
  296.8 111.3 %all-reduce.13.cloned.1.call-done = f32[512,256]{1,0:T(8,128)} async-done(((f32[512,256]{1,0:T(8,128)}), f32[512,256]{1,0:T(8,128)}) %all-reduce.13.cloned.1.call-update) | async-done | bytes 524304 | tf_op jit(solution)/shard_map/psum | solution.py:26
  414.6 110.1 %all-reduce.15.cloned.1.call-done = f32[256,256]{0,1:T(8,128)} async-done(((f32[256,256]{0,1:T(8,128)}), f32[256,256]{0,1:T(8,128)}) %all-reduce.15.cloned.1.call-update) | async-done | bytes 262160 | tf_op jit(solution)/shard_map/psum | solution.py:26
  527.5 11.7 %cholesky.248 = f32[128,128]{1,0:T(8,128)S(1)} custom-call(f32[128,128]{1,0:T(8,128)S(1)} %cholesky.349), custom_call_target="Cholesky" | custom-call | tf_op jit(solution)/shard_map/jit(cholesky)/cholesky | solution.py:30
  539.3 9.8 custom-call.18
  551.3 11.7 %cholesky.265 = f32[128,128]{1,0:T(8,128)S(1)} custom-call(f32[128,128]{1,0:T(8,128)S(1)} %convolution_subtract_fusion.2), custom_call_target="Cholesky" | custom-call | tf_op jit(solution)/shard_map/jit(cholesky)/cholesky | solution.py:30
  566.5 4.1 while.7
  571.2 20.5 %custom-call.19 = f32[2,128,128]{1,2,0:T(8,128)S(1)} custom-call(f32[2,128,128]{2,1,0:T(8,128)} %copy-done.19), custom_call_target="InvertDiagBlocksLowerTriangular" | custom-call | tf_op jit(solution)/shard_map/triangular_solve/custom-call.0 | solution.py:31
  594.1 4.3 fusion.14
  598.4 111.3 %all-reduce.17.cloned.1.call-done = f32[512,256]{1,0:T(8,128)} async-done(((f32[512,256]{1,0:T(8,128)}), f32[512,256]{1,0:T(8,128)}) %all-reduce.17.cloned.1.call-update) | async-done | bytes 524304 | tf_op jit(solution)/shard_map/psum | solution.py:26
  709.7 3.5 fusion.88
  716.2 110.1 %all-reduce.19.cloned.1.call-done = f32[256,256]{0,1:T(8,128)} async-done(((f32[256,256]{0,1:T(8,128)}), f32[256,256]{0,1:T(8,128)}) %all-reduce.19.cloned.1.call-update) | async-done | bytes 262160 | tf_op jit(solution)/shard_map/psum | solution.py:26
  829.1 11.7 %cholesky.282 = f32[128,128]{1,0:T(8,128)S(1)} custom-call(f32[128,128]{1,0:T(8,128)S(1)} %cholesky.352), custom_call_target="Cholesky" | custom-call | tf_op jit(solution)/shard_map/jit(cholesky)/cholesky | solution.py:30
  840.9 9.8 custom-call.20
  852.9 11.7 %cholesky.299 = f32[128,128]{1,0:T(8,128)S(1)} custom-call(f32[128,128]{1,0:T(8,128)S(1)} %convolution_subtract_fusion.1), custom_call_target="Cholesky" | custom-call | tf_op jit(solution)/shard_map/jit(cholesky)/cholesky | solution.py:30
  868.1 3.9 while.8
  872.6 20.7 %custom-call.21 = f32[2,128,128]{1,2,0:T(8,128)S(1)} custom-call(f32[2,128,128]{2,1,0:T(8,128)} %copy-done.20), custom_call_target="InvertDiagBlocksLowerTriangular" | custom-call | tf_op jit(solution)/shard_map/triangular_solve/custom-call.0 | solution.py:31
  896.4 4.3 fusion.19
  900.8 111.3 %all-reduce.21.cloned.1.call-done = f32[512,256]{1,0:T(8,128)} async-done(((f32[512,256]{1,0:T(8,128)}), f32[512,256]{1,0:T(8,128)}) %all-reduce.21.cloned.1.call-update) | async-done | bytes 524304 | tf_op jit(solution)/shard_map/psum | solution.py:26
  1016.8 11.7 %cholesky.316 = f32[128,128]{1,0:T(8,128)S(1)} custom-call(f32[128,128]{1,0:T(8,128)S(1)} %cholesky.355), custom_call_target="Cholesky" | custom-call | tf_op jit(solution)/shard_map/jit(cholesky)/cholesky | solution.py:39
  1028.6 10.0 custom-call.22
  1040.7 11.7 %cholesky.333 = f32[128,128]{1,0:T(8,128)S(1)} custom-call(f32[128,128]{1,0:T(8,128)S(1)} %convolution_subtract_fusion), custom_call_target="Cholesky" | custom-call | tf_op jit(solution)/shard_map/jit(cholesky)/cholesky | solution.py:39
  (152 shorter events, 81.6 us)
Async XLA Ops:
  6.5 1.7 copy-start
  6.5 52.3 %all-reduce.9.cloned.1.call-start = ((), (), s32[]{:S(2)}) async-start(), calls=%async_computation | async-start | bytes 262144 | tf_op jit(solution)/shard_map/psum | solution.py:57
  6.5 2.4 copy-start.10
  10.4 213.3 %all-reduce.11.cloned.1.call-start = ((), (), s32[]{:S(2)}) async-start(), calls=%async_computation.1 | async-start | bytes 524288 | tf_op jit(solution)/shard_map/psum | solution.py:26
  67.5 1.3 copy-start.9
  67.5 10.9 %collective-permute-start = (f32[1024,128]{1,0:T(8,128)S(1)}, f32[1024,128]{1,0:T(8,128)}, u32[]{:S(2)}, u32[]{:S(2)}) collective-permute-start(f32[1024,128]{1,0:T(8,128)S(1)} %bitcast.167), channel_id=1, source_target_pairs={{0,4},{4,0},{8,12},{12,8},{1,5},{5,1},{9,13},{13,9},{2,6},{6,2},{1... | collective-permute-start | bytes 1572872 | tf_op jit(solution)/shard_map/ppermute | solution.py:18
  80.0 22.8 %collective-permute-start.1 = (f32[1024,256]{1,0:T(8,128)S(1)}, f32[1024,256]{1,0:T(8,128)}, u32[]{:S(2)}, u32[]{:S(2)}) collective-permute-start(f32[1024,256]{1,0:T(8,128)S(1)} %maximum_select_fusion.1), channel_id=1, source_target_pairs={{0,8},{8,0},{4,12},{12,4},{1,9},{9,1},{5,13},{13,5},{2,10},{10,2},... | collective-permute-start | bytes 3145736 | tf_op jit(solution)/shard_map/ppermute | solution.py:18
  104.8 1.4 copy-start.1
  108.8 299.3 %all-reduce.13.cloned.1.call-start = ((), (), s32[]{:S(2)}) async-start(), calls=%async_computation.2 | async-start | bytes 1048576 | tf_op jit(solution)/shard_map/psum | solution.py:26
  225.7 0.7 copy-start.15
  262.0 1.8 copy-start.11
  269.0 0.7 copy-start.18
  290.1 2.3 copy-start.2
  296.8 228.0 %all-reduce.15.cloned.1.call-start = ((), (), s32[]{:S(2)}) async-start(), calls=%async_computation.3 | async-start | bytes 524288 | tf_op jit(solution)/shard_map/psum | solution.py:26
  414.1 295.6 %all-reduce.17.cloned.1.call-start = ((), (), s32[]{:S(2)}) async-start(), calls=%async_computation.4 | async-start | bytes 1048576 | tf_op jit(solution)/shard_map/psum | solution.py:26
  526.8 0.7 copy-start.16
  563.0 2.5 copy-start.12
  570.6 0.7 copy-start.19
  591.7 2.3 copy-start.3
  598.4 227.9 %all-reduce.19.cloned.1.call-start = ((), (), s32[]{:S(2)}) async-start(), calls=%async_computation.5 | async-start | bytes 524288 | tf_op jit(solution)/shard_map/psum | solution.py:26
  715.7 296.4 %all-reduce.21.cloned.1.call-start = ((), (), s32[]{:S(2)}) async-start(), calls=%async_computation.6 | async-start | bytes 1048576 | tf_op jit(solution)/shard_map/psum | solution.py:26
  828.4 0.7 copy-start.17
  864.6 2.5 copy-start.13
  872.0 0.7 copy-start.20
  893.3 3.1 copy-start.4
  894.0 1.7 copy-start.5
  895.6 0.8 copy-start.7
  900.7 154.5 %copy-start.6 = (f32[128,1024]{1,0:T(8,128)S(1)}, f32[128,1024]{1,0:T(8,128)}, u32[]{:S(2)}) copy-start(f32[128,1024]{1,0:T(8,128)} %copy-done.5) | copy-start | bytes 1572868
  900.7 154.5 %copy-start.8 = (f32[1024,128]{0,1:T(8,128)S(1)}, f32[1024,128]{0,1:T(8,128)}, u32[]{:S(2)}) copy-start(f32[1024,128]{0,1:T(8,128)} %copy-done.7) | copy-start | bytes 1572868
  1016.1 0.7 copy-start.14
Sparse Core Ops, SparseCore 0:
  10.5 48.2 all-reduce.8
  108.9 114.7 all-reduce.10
  296.9 111.1 all-reduce.12
  414.3 110.4 all-reduce.14
  598.5 111.1 all-reduce.16
  715.8 110.4 all-reduce.18
  900.9 111.1 all-reduce.20
where the time goes:
time: 1070 us; the launch traced here: 1060 us
  waiting for transfers between devices  747 us (70%)
  other arithmetic  211 us (20%)
  matrix products  53.8 us (5%)
  local copies, waits for them, and re-layouts  27.5 us (3%)
  between operations  19.2 us (2%)
    psum x6, waiting for transfers between devices, layer_total(): return lax.psum(value, 'pipe')  669 us
    another operation x20, other arithmetic, orthonormal(): lower = jnp.linalg.cholesky(total(mm(block.T, block)))  103 us
    another operation x7, other arithmetic, orthonormal(): lax.linalg.triangular_solve(lower, block, left_side=False, lower=True, tr...  64.6 us
    psum x1, waiting for transfers between devices, shards(): both = lax.psum(jnp.concatenate([left_part, right_part], axis=1), 'tensor')  48.4 us
    another operation x7, other arithmetic, reduce_plain(): lower = jnp.linalg.cholesky(mm(weights.T, weights))  34.8 us
    dot_general x10, matrix products, mm(): return jnp.matmul(a, b, precision=lax.Precision.HIGHEST)  30.7 us
    ppermute x2, waiting for transfers between devices, from_partner(): return lax.ppermute(block, axis, route)  29.7 us
  transfers between devices with their start and end apart: 9, of which 9 were waited for; matrix products, arithmetic and copies ran while one was open for 0% of the time, Pallas kernels for 0%

commit v1 on v0

--- a/solution.py
+++ b/solution.py
@@ -23,7 +23,7 @@
 
 
 def layer_total(value):
-    return lax.psum(value, "pipe")
+    return jnp.sum(lax.all_gather(value, "pipe"), axis=0)
 
 
 def orthonormal(block, total):

time: 1070 us -> 708 us (0.66)
  waiting for transfers between devices: 747 us -> 369 us
  other arithmetic: 211 us -> 232 us
    psum x6 -> x0, waiting for transfers between devices: 669 us -> none  [layer_total(): return lax.psum(value, 'pipe')]
    all_gather x0 -> x6, waiting for transfers between devices: none -> 291 us  [layer_total(): return jnp.sum(lax.all_gather(value, 'pipe'), axis=0)]
    reduce_sum x0 -> x6, other arithmetic: none -> 21 us  [layer_total(): return jnp.sum(lax.all_gather(value, 'pipe'), axis=0)]
where the time goes in v1:
time: 708 us; the launch traced here: 700 us
  waiting for transfers between devices  369 us (52%)
  other arithmetic  232 us (33%)
  matrix products  49.9 us (7%)
  local copies, waits for them, and re-layouts  24.5 us (3%)
  between operations  19.4 us (3%)
    all_gather x6, waiting for transfers between devices, layer_total(): return jnp.sum(lax.all_gather(value, 'pipe'), axis=0)  291 us
    another operation x20, other arithmetic, orthonormal(): lower = jnp.linalg.cholesky(total(mm(block.T, block)))  103 us
    another operation x7, other arithmetic, orthonormal(): lax.linalg.triangular_solve(lower, block, left_side=False, lower=True, tr...  64.6 us
    psum x1, waiting for transfers between devices, shards(): both = lax.psum(jnp.concatenate([left_part, right_part], axis=1), 'tensor')  48.4 us
    another operation x7, other arithmetic, reduce_plain(): lower = jnp.linalg.cholesky(mm(weights.T, weights))  34.8 us
    ppermute x2, waiting for transfers between devices, from_partner(): return lax.ppermute(block, axis, route)  29.6 us
    dot_general x10, matrix products, mm(): return jnp.matmul(a, b, precision=lax.Precision.HIGHEST)  28.2 us
    reduce_sum x6, other arithmetic, layer_total(): return jnp.sum(lax.all_gather(value, 'pipe'), axis=0)  21 us
  transfers between devices with their start and end apart: 9, of which 9 were waited for; matrix products, arithmetic and copies ran while one was open for 0% of the time, Pallas kernels for 0%

profile of v1, /device:TPU:1, one launch (start us, length us, event | category | flops | bytes accessed | tf_op | source)
XLA Modules:
  0.0 700.2 jit_solution(6892811302131039061)
XLA Ops:
  10.4 48.4 %all-reduce.3.cloned.1.call-done = f32[512,64]{0,1:T(8,128)} async-done(((f32[512,64]{0,1:T(8,128)}), f32[512,64]{0,1:T(8,128)}) %all-reduce.3.cloned.1.call-update) | async-done | bytes 131088 | tf_op jit(solution)/shard_map/psum | solution.py:57
  66.0 9.5 %collective-permute-done = f32[1024,128]{1,0:T(8,128)S(1)} collective-permute-done((f32[1024,128]{1,0:T(8,128)S(1)}, f32[1024,128]{1,0:T(8,128)S(1)}, u32[]{:S(2)}, u32[]{:S(2)}) %collective-permute-start) | collective-permute-done | bytes 524320 | tf_op jit(solution)/shard_map/ppermute | solution.py:18
  79.6 20.0 %collective-permute-done.1 = f32[1024,256]{1,0:T(8,128)} collective-permute-done((f32[1024,256]{1,0:T(8,128)S(1)}, f32[1024,256]{1,0:T(8,128)}, u32[]{:S(2)}, u32[]{:S(2)}) %collective-permute-start.1) | collective-permute-done | bytes 1048608 | tf_op jit(solution)/shard_map/ppermute | solution.py:18
  104.5 46.9 %all-gather.13.cloned.1.call-done = f32[4096,256]{1,0:T(8,128)} async-done(((f32[256,256]{1,0:T(8,128)}), f32[4096,256]{1,0:T(8,128)}) %all-gather.13.cloned.1.call-update) | async-done | bytes 4194320 | tf_op jit(solution)/shard_map/all_gather | solution.py:26
  156.4 11.7 %cholesky.214 = f32[128,128]{1,0:T(8,128)S(1)} custom-call(f32[128,128]{1,0:T(8,128)S(1)} %cholesky.346), custom_call_target="Cholesky" | custom-call | tf_op jit(solution)/shard_map/jit(cholesky)/cholesky | solution.py:30
  168.2 9.8 %custom-call.16 = f32[1,128,128]{1,2,0:T(8,128)S(1)} custom-call(f32[1,128,128]{2,1,0:T(8,128)S(1)} %get-tuple-element.79), custom_call_target="InvertDiagBlocksLowerTriangular" | custom-call | tf_op jit(solution)/shard_map/jit(cholesky)/cholesky | solution.py:30
  180.1 11.7 %cholesky.231 = f32[128,128]{1,0:T(8,128)S(1)} custom-call(f32[128,128]{1,0:T(8,128)S(1)} %convolution_subtract_fusion.3), custom_call_target="Cholesky" | custom-call | tf_op jit(solution)/shard_map/jit(cholesky)/cholesky | solution.py:30
  194.9 4.3 while.6
  199.9 20.5 %custom-call.17 = f32[2,128,128]{1,2,0:T(8,128)S(1)} custom-call(f32[2,128,128]{2,1,0:T(8,128)} %copy-done.15), custom_call_target="InvertDiagBlocksLowerTriangular" | custom-call | tf_op jit(solution)/shard_map/triangular_solve/custom-call.0 | solution.py:31
  222.7 4.3 fusion.10
  227.0 54.5 %all-gather.15.cloned.1.call-done = f32[8192,256]{1,0:T(8,128)} async-done(((f32[512,256]{1,0:T(8,128)}), f32[8192,256]{1,0:T(8,128)}) %all-gather.15.cloned.1.call-update) | async-done | bytes 8388624 | tf_op jit(solution)/shard_map/all_gather | solution.py:26
  281.5 4.8 reduce_sum.55
  292.2 40.1 %all-gather.17.cloned.1.call-done = f32[4096,256]{1,0:T(8,128)} async-done(((f32[256,256]{1,0:T(8,128)}), f32[4096,256]{1,0:T(8,128)}) %all-gather.17.cloned.1.call-update) | async-done | bytes 4194320 | tf_op jit(solution)/shard_map/all_gather | solution.py:26
  337.3 11.7 %cholesky.248 = f32[128,128]{1,0:T(8,128)S(1)} custom-call(f32[128,128]{1,0:T(8,128)S(1)} %cholesky.349), custom_call_target="Cholesky" | custom-call | tf_op jit(solution)/shard_map/jit(cholesky)/cholesky | solution.py:30
  349.1 9.8 %custom-call.18 = f32[1,128,128]{1,2,0:T(8,128)S(1)} custom-call(f32[1,128,128]{2,1,0:T(8,128)S(1)} %get-tuple-element.75), custom_call_target="InvertDiagBlocksLowerTriangular" | custom-call | tf_op jit(solution)/shard_map/jit(cholesky)/cholesky | solution.py:30
  361.1 11.7 %cholesky.265 = f32[128,128]{1,0:T(8,128)S(1)} custom-call(f32[128,128]{1,0:T(8,128)S(1)} %convolution_subtract_fusion.2), custom_call_target="Cholesky" | custom-call | tf_op jit(solution)/shard_map/jit(cholesky)/cholesky | solution.py:30
  376.5 4.2 while.7
  381.4 20.5 %custom-call.19 = f32[2,128,128]{1,2,0:T(8,128)S(1)} custom-call(f32[2,128,128]{2,1,0:T(8,128)} %copy-done.16), custom_call_target="InvertDiagBlocksLowerTriangular" | custom-call | tf_op jit(solution)/shard_map/triangular_solve/custom-call.0 | solution.py:31
  404.1 4.3 fusion.14
  408.5 54.5 %all-gather.19.cloned.1.call-done = f32[8192,256]{1,0:T(8,128)} async-done(((f32[512,256]{1,0:T(8,128)}), f32[8192,256]{1,0:T(8,128)}) %all-gather.19.cloned.1.call-update) | async-done | bytes 8388624 | tf_op jit(solution)/shard_map/all_gather | solution.py:26
  463.0 4.8 reduce_sum.57
  473.7 40.1 %all-gather.21.cloned.1.call-done = f32[4096,256]{1,0:T(8,128)} async-done(((f32[256,256]{1,0:T(8,128)}), f32[4096,256]{1,0:T(8,128)}) %all-gather.21.cloned.1.call-update) | async-done | bytes 4194320 | tf_op jit(solution)/shard_map/all_gather | solution.py:26
  518.8 11.7 %cholesky.282 = f32[128,128]{1,0:T(8,128)S(1)} custom-call(f32[128,128]{1,0:T(8,128)S(1)} %cholesky.352), custom_call_target="Cholesky" | custom-call | tf_op jit(solution)/shard_map/jit(cholesky)/cholesky | solution.py:30
  530.6 9.8 %custom-call.20 = f32[1,128,128]{1,2,0:T(8,128)S(1)} custom-call(f32[1,128,128]{2,1,0:T(8,128)S(1)} %get-tuple-element.71), custom_call_target="InvertDiagBlocksLowerTriangular" | custom-call | tf_op jit(solution)/shard_map/jit(cholesky)/cholesky | solution.py:30
  542.6 11.7 %cholesky.299 = f32[128,128]{1,0:T(8,128)S(1)} custom-call(f32[128,128]{1,0:T(8,128)S(1)} %convolution_subtract_fusion.1), custom_call_target="Cholesky" | custom-call | tf_op jit(solution)/shard_map/jit(cholesky)/cholesky | solution.py:30
  558.0 4.1 while.8
  562.7 20.7 %custom-call.21 = f32[2,128,128]{1,2,0:T(8,128)S(1)} custom-call(f32[2,128,128]{2,1,0:T(8,128)} %copy-done.17), custom_call_target="InvertDiagBlocksLowerTriangular" | custom-call | tf_op jit(solution)/shard_map/triangular_solve/custom-call.0 | solution.py:31
  586.5 4.2 fusion.19
  590.8 54.6 %all-gather.23.cloned.1.call-done = f32[8192,256]{1,0:T(8,128)} async-done(((f32[512,256]{1,0:T(8,128)}), f32[8192,256]{1,0:T(8,128)}) %all-gather.23.cloned.1.call-update) | async-done | bytes 8388624 | tf_op jit(solution)/shard_map/all_gather | solution.py:26
  652.9 11.7 %cholesky.316 = f32[128,128]{1,0:T(8,128)S(1)} custom-call(f32[128,128]{1,0:T(8,128)S(1)} %cholesky.355), custom_call_target="Cholesky" | custom-call | tf_op jit(solution)/shard_map/jit(cholesky)/cholesky | solution.py:39
  664.6 10.0 %custom-call.22 = f32[1,128,128]{1,2,0:T(8,128)S(1)} custom-call(f32[1,128,128]{2,1,0:T(8,128)S(1)} %get-tuple-element.67), custom_call_target="InvertDiagBlocksLowerTriangular" | custom-call | tf_op jit(solution)/shard_map/jit(cholesky)/cholesky | solution.py:39
  676.8 11.7 %cholesky.333 = f32[128,128]{1,0:T(8,128)S(1)} custom-call(f32[128,128]{1,0:T(8,128)S(1)} %convolution_subtract_fusion), custom_call_target="Cholesky" | custom-call | tf_op jit(solution)/shard_map/jit(cholesky)/cholesky | solution.py:39
  (152 shorter events, 94.3 us)
Async XLA Ops:
  6.5 1.7 copy-start
  6.5 52.3 %all-reduce.3.cloned.1.call-start = ((), (), s32[]{:S(2)}) async-start(), calls=%async_computation | async-start | bytes 262144 | tf_op jit(solution)/shard_map/psum | solution.py:57
  6.5 2.4 copy-start.7
  10.4 141.0 %all-gather.13.cloned.1.call-start = ((), (), s32[]{:S(2)}) async-start(), calls=%async_computation.1 | async-start | bytes 4456448 | tf_op jit(solution)/shard_map/all_gather | solution.py:26
  64.7 1.3 copy-start.6
  64.7 10.8 %collective-permute-start = (f32[1024,128]{1,0:T(8,128)S(1)}, f32[1024,128]{1,0:T(8,128)S(1)}, u32[]{:S(2)}, u32[]{:S(2)}) collective-permute-start(f32[1024,128]{1,0:T(8,128)S(1)} %bitcast.179), channel_id=1, source_target_pairs={{0,4},{4,0},{8,12},{12,8},{1,5},{5,1},{9,13},{13,9},{2,6},{6,2},{1... | collective-permute-start | bytes 1572872 | tf_op jit(solution)/shard_map/ppermute | solution.py:18
  76.8 22.8 %collective-permute-start.1 = (f32[1024,256]{1,0:T(8,128)S(1)}, f32[1024,256]{1,0:T(8,128)}, u32[]{:S(2)}, u32[]{:S(2)}) collective-permute-start(f32[1024,256]{1,0:T(8,128)S(1)} %maximum_select_fusion.1), channel_id=1, source_target_pairs={{0,8},{8,0},{4,12},{12,4},{1,9},{9,1},{5,13},{13,5},{2,10},{10,2},... | collective-permute-start | bytes 3145736 | tf_op jit(solution)/shard_map/ppermute | solution.py:18
  104.2 177.3 %all-gather.15.cloned.1.call-start = ((), (), s32[]{:S(2)}) async-start(), calls=%async_computation.2 | async-start | bytes 8912896 | tf_op jit(solution)/shard_map/all_gather | solution.py:26
  155.7 0.7 copy-start.12
  191.9 2.0 copy-start.8
  199.2 0.6 copy-start.15
  227.0 105.4 %all-gather.17.cloned.1.call-start = ((), (), s32[]{:S(2)}) async-start(), calls=%async_computation.3 | async-start | bytes 4456448 | tf_op jit(solution)/shard_map/all_gather | solution.py:26
  291.8 171.3 %all-gather.19.cloned.1.call-start = ((), (), s32[]{:S(2)}) async-start(), calls=%async_computation.4 | async-start | bytes 8912896 | tf_op jit(solution)/shard_map/all_gather | solution.py:26
  336.6 0.7 copy-start.13
  372.8 2.6 copy-start.9
  380.7 0.6 copy-start.16
  408.5 105.4 %all-gather.21.cloned.1.call-start = ((), (), s32[]{:S(2)}) async-start(), calls=%async_computation.5 | async-start | bytes 4456448 | tf_op jit(solution)/shard_map/all_gather | solution.py:26
  473.3 172.1 %all-gather.23.cloned.1.call-start = ((), (), s32[]{:S(2)}) async-start(), calls=%async_computation.6 | async-start | bytes 8912896 | tf_op jit(solution)/shard_map/all_gather | solution.py:26
  518.1 0.7 copy-start.14
  554.3 2.6 copy-start.10
  562.0 0.6 copy-start.17
  584.0 1.7 copy-start.2
  585.6 0.8 copy-start.4
  649.3 42.0 %copy-start.3 = (f32[128,1024]{1,0:T(8,128)S(1)}, f32[128,1024]{1,0:T(8,128)}, u32[]{:S(2)}) copy-start(f32[128,1024]{1,0:T(8,128)} %copy-done.2) | copy-start | bytes 1572868
  649.3 42.0 %copy-start.5 = (f32[1024,128]{0,1:T(8,128)S(1)}, f32[1024,128]{0,1:T(8,128)}, u32[]{:S(2)}) copy-start(f32[1024,128]{0,1:T(8,128)} %copy-done.4) | copy-start | bytes 1572868
  650.3 42.8 %copy-start.1 = (bf16[1,512,2048]{2,1,0:T(8,128)(2,1)S(1)}, bf16[1,512,2048]{2,1,0:T(8,128)(2,1)}, u32[]{:S(2)}) copy-start(bf16[1,512,2048]{2,1,0:T(8,128)(2,1)} %param.7) | copy-start | bytes 6291460
  652.2 0.7 copy-start.11
Sparse Core Ops, SparseCore 0:
  10.5 48.2 all-reduce.2
  104.4 46.9 all-gather.12
  227.1 54.4 all-gather.14
  291.9 40.4 all-gather.16
  408.6 54.4 all-gather.18
  473.4 40.4 all-gather.20
  590.9 54.3 all-gather.22
